TPU v7x, 256 devices: a whole 4x4x8 slice. The times are simulated.
256 devices in a mesh: vert: 128 (over y_hi, x, z, core), sa: 2 (over y_lo).
Axes of the slice: x: 4, y: 4 (y_hi: 2, y_lo: 2; y = y_hi * 2 + y_lo), z: 8, core: 2. Of those that a mesh axis runs over, the one named last changes fastest.
Arguments:
- state: bfloat16 [2048, 32, 1024], P('vert', 'sa'), may hold values from -6 to 6
- cotangent: bfloat16 [2048, 32, 1024], P('vert', 'sa'), may hold values from -6 to 6
- collision: bfloat16 [2048, 2048], replicated, may hold values from -0.125 to 0.125
- wall_shape: float32 [2048], replicated, may hold values from 0.5 to 2
- flux_weight: float32 [2048], replicated, may hold values from -0.125 to 0.125
- courant: float32 [3, 2048], P(None, 'vert'), may hold values from 0.03 to 0.3
- upwind_bits: int32 [3, 2048], P(None, 'vert'), may hold values from 0 to 1
- accommodation: float32 [256, 128], P(('vert', 'sa')), may hold values from 0.2 to 1
- wall_flags: int32 [256, 128], P(('vert', 'sa')), may hold values 0 or 1
Outputs:
- advanced: bfloat16 [2048, 32, 1024], P('vert', 'sa')
- previous: bfloat16 [2048, 32, 1024], P('vert', 'sa')
- sensitivity: float32 [256, 128], P(('vert', 'sa'))
All inputs are finite; a program needn't handle non-finite values. No bound on the sum of `wall_flags` on one device may be relied on, other than what follows from the above.
Results may differ from a plain program's by a relative error of at most 0.0051.
Values may be sent and summed in bfloat16 or wider, within the bound.
A program may use at most 64 MiB of HBM per device.

v0:
```python
import jax
import jax.numpy as jnp
from jax import lax
from jax.sharding import PartitionSpec as P

NZ = 32


def padded_2(shard, sides, width):
    for axis, dim in sides:
        size, length = (lax.axis_size(axis), shard.shape[dim])
        up = [(i, (i + 1) % size) for i in range(size - 1)]
        down = [(j, i) for i, j in up]
        last = lax.slice_in_dim(shard, length - width, length, axis=dim)
        first = lax.slice_in_dim(shard, 0, width, axis=dim)
        before = lax.ppermute(last, axis, up)
        after = lax.ppermute(first, axis, down)
        shard = jnp.concatenate([before, shard, after], axis=dim)
    return shard


def neighbour_pairs(padded, z_cells):
    middle = padded[:, 1:-1]
    plane_len = middle.shape[2]
    z_index = lax.broadcasted_iota(jnp.int32, (1, 1, plane_len), 2) % z_cells
    wide_y = jnp.pad(middle, ((0, 0), (0, 0), (z_cells, z_cells)))
    wide_z = jnp.pad(middle, ((0, 0), (0, 0), (1, 1)))
    zero_val = jnp.zeros((), middle.dtype)
    minus_side = (
        padded[:, :-2],
        wide_y[:, :, :plane_len],
        jnp.where(z_index != 0, wide_z[:, :, :plane_len], zero_val),
    )
    plus_side = (
        padded[:, 2:],
        wide_y[:, :, 2 * z_cells :],
        jnp.where(z_index != z_cells - 1, wide_z[:, :, 2:], zero_val),
    )
    return (middle, minus_side, plus_side)


def transport(padded, courant, upwind, z_cells, forward):
    middle, minus_side, plus_side = neighbour_pairs(padded, z_cells)
    central = middle.astype(jnp.float32)
    result = central
    for axis_num in range(3):
        speed_ratio = courant[axis_num][:, None, None]
        upward = upwind[axis_num][:, None, None] == 1
        if forward:
            donor = jnp.where(upward, minus_side[axis_num], plus_side[axis_num])
        else:
            donor = jnp.where(upward, plus_side[axis_num], minus_side[axis_num])
        result = result - speed_ratio * (central - donor.astype(jnp.float32))
    return result


def collide_forward(passed, collision, wall_shape, flux_weight, gain):
    moved = passed.astype(jnp.float32)
    density = jnp.sum(flux_weight[:, None] * moved, axis=0, keepdims=True)
    target = wall_shape[:, None] * density - moved
    relaxed = moved + gain * target
    relaxed_half = relaxed.astype(jnp.bfloat16)
    mixed = lax.dot_general(
        collision, relaxed_half, (((0,), (0,)), ((), ())), preferred_element_type=jnp.float32
    )
    advanced = (relaxed + mixed).astype(jnp.bfloat16)
    return (advanced, target)


def collide_adjoint(adjoint_in, collision, wall_shape, flux_weight, gain, flags_row, target):
    adjoint_h = adjoint_in.astype(jnp.float32) + jnp.dot(
        collision, adjoint_in, preferred_element_type=jnp.float32
    )
    weighted = jnp.sum(wall_shape[:, None] * adjoint_h, axis=0, keepdims=True)
    adjoint_g = (adjoint_h + gain * (flux_weight[:, None] * weighted - adjoint_h)).astype(
        jnp.bfloat16
    )
    sensitivity = flags_row * jnp.sum(adjoint_h * target, axis=0, keepdims=True)
    return (adjoint_g, sensitivity)


def body(
    state,
    cotangent,
    collision,
    wall_shape,
    flux_weight,
    courant,
    upwind_bits,
    accommodation,
    wall_flags,
):
    local_vel, slab, plane_len = state.shape
    sub_cells = slab * plane_len
    padded = padded_2(state, (("sa", 1),), 1)
    passed = transport(padded, courant, upwind_bits, NZ, True).astype(jnp.bfloat16)
    flat_passed = passed.reshape(local_vel, sub_cells)
    flat_cot = cotangent.reshape(local_vel, sub_cells)
    flags_row = wall_flags.astype(jnp.float32)
    gain = accommodation * flags_row
    cell_state = lax.all_to_all(flat_passed, "vert", split_axis=1, concat_axis=0, tiled=True)
    advanced, target = collide_forward(cell_state, collision, wall_shape, flux_weight, gain)
    back_state = lax.all_to_all(advanced, "vert", split_axis=0, concat_axis=1, tiled=True)
    cell_cot = lax.all_to_all(flat_cot, "vert", split_axis=1, concat_axis=0, tiled=True)
    adjoint_g, sensitivity = collide_adjoint(
        cell_cot, collision, wall_shape, flux_weight, gain, flags_row, target
    )
    back_adjoint = lax.all_to_all(adjoint_g, "vert", split_axis=0, concat_axis=1, tiled=True)
    back_state = back_state.reshape(local_vel, slab, plane_len)
    back_adjoint = back_adjoint.reshape(local_vel, slab, plane_len)
    adjoint_pad = padded_2(back_adjoint, (("sa", 1),), 1)
    previous = transport(adjoint_pad, courant, upwind_bits, NZ, False).astype(jnp.bfloat16)
    return (back_state, previous, sensitivity)


def solution(mesh):
    return jax.shard_map(
        body,
        mesh=mesh,
        in_specs=(
            P("vert", "sa", None),
            P("vert", "sa", None),
            P(),
            P(),
            P(),
            P(None, "vert"),
            P(None, "vert"),
            P(("vert", "sa"), None),
            P(("vert", "sa"), None),
        ),
        out_specs=(P("vert", "sa", None), P("vert", "sa", None), P(("vert", "sa"), None)),
        check_vma=False,
    )
```

profile of v0, /device:TPU:1, one launch (start us, length us, event | category | flops | bytes accessed | tf_op | source)
XLA Modules:
  0.0 137.5 jit_solution(18100484792520479977)
XLA Ops:
  0.6 1.3 all_to_all.53
  1.9 1.1 copy.39
  3.0 16.4 %all-to-all-start.2 = ((bf16[16,128,128]{2,0,1:T(8,128)(2,1)}), bf16[16,128,128]{2,0,1:T(8,128)(2,1)S(1)}, u32[]{:S(2)}, u32[]{:S(2)}) async-start(bf16[16,128,128]{2,0,1:T(8,128)(2,1)} %copy.39), calls=%async_computation.2 | async-start | bytes 1048576 | tf_op jit(solution)/shard_map/all_to_all | solution.py:104
  19.4 1.1 fusion.36
  20.6 2.3 %collective-permute-start = (bf16[16,1,1024]{2,1,0:T(2,128)(2,1)S(1)}, bf16[16,1,1024]{2,1,0:T(2,128)(2,1)S(1)}, u32[]{:S(2)}, u32[]{:S(2)}) collective-permute-start(bf16[16,1,1024]{2,1,0:T(2,128)(2,1)S(1)} %get-tuple-element.7), channel_id=1, source_target_pairs={{0,1},{2,3},{4,5},{6,7},{8,9},{10,11},{12,13},{14,15},{16,17},{18,... | collective-permute-start | bytes 98312 | tf_op jit(solution)/shard_map/ppermute | solution.py:16
  22.9 1.3 collective-permute-start.1
  25.8 2.8 %collective-permute-done.1 = bf16[16,1,1024]{2,1,0:T(2,128)(2,1)S(1)} collective-permute-done((bf16[16,1,1024]{2,1,0:T(2,128)(2,1)S(1)}, bf16[16,1,1024]{2,1,0:T(2,128)(2,1)S(1)}, u32[]{:S(2)}, u32[]{:S(2)}) %collective-permute-start.1) | collective-permute-done | bytes 32800 | tf_op jit(solution)/shard_map/ppermute | solution.py:17
  28.6 5.1 %fusion.5 = bf16[16,16,1024]{2,1,0:T(8,128)(2,1)S(1)} fusion(bf16[16,16,1024]{2,1,0:T(8,128)(2,1)} %param.9, bf16[16,1,1024]{2,1,0:T(2,128)(2,1)S(1)} %collective-permute-done.1, bf16[16,1,1024]{2,1,0:T(2,128)(2,1)S(1)} %collective-permute-done, f32[16]{0:T(128)S(1)} %get-tuple-element.13, f32[16]{0:T(128)S(1)} %get-tuple-element.14, ...), kind=kLoop, calls=%fused_computation.15 | loop fusion | flops 7077888 | bytes 1116400 | tf_op jit(solution)/shard_map/convert_element_type | solution.py:96
  33.9 1.1 copy.34
  35.1 4.3 %all-to-all-done.2 = bf16[16,128,128]{2,0,1:T(8,128)(2,1)S(1)} async-done(((bf16[16,128,128]{2,0,1:T(8,128)(2,1)}), bf16[16,128,128]{2,0,1:T(8,128)(2,1)S(1)}, u32[]{:S(2)}, u32[]{:S(2)}) %all-to-all-start.2) | async-done | bytes 524320 | tf_op jit(solution)/shard_map/all_to_all | solution.py:104
  39.4 11.6 %all-to-all-start = ((bf16[16,128,128]{2,0,1:T(8,128)(2,1)}), bf16[16,128,128]{2,0,1:T(8,128)(2,1)S(1)}, u32[]{:S(2)}, u32[]{:S(2)}) async-start(bf16[16,128,128]{2,0,1:T(8,128)(2,1)} %copy.34), calls=%async_computation | async-start | bytes 1048576 | tf_op jit(solution)/shard_map/all_to_all | solution.py:101
  51.8 1.0 copy.40
  52.8 18.2 %all-to-all-done = bf16[16,128,128]{2,0,1:T(8,128)(2,1)S(1)} async-done(((bf16[16,128,128]{2,0,1:T(8,128)(2,1)}), bf16[16,128,128]{2,0,1:T(8,128)(2,1)S(1)}, u32[]{:S(2)}, u32[]{:S(2)}) %all-to-all-start) | async-done | bytes 524320 | tf_op jit(solution)/shard_map/all_to_all | solution.py:101
  71.7 6.6 %multiply_reduce_fusion = (f32[128]{0:T(128)S(1)}, f32[128]{0:T(128)S(1)}, f32[2048,128]{0,1:T(8,128)S(1)}) fusion(f32[2048,128]{0,1:T(8,128)S(1)} %copy.36, f32[128]{0:T(128)S(1)} %fusion.14, f32[2048]{0:T(1024)S(1)} %copy-done, bf16[2048,2048]{1,0:T(8,128)(2,1)} %param.11, bf16[2048,128]{1,0:T(8,128)(2,1)S(1)} %bitcast.39, bf16[2048,128]{0,1:T(8,128)(2,1)} %copy.40), kind=kOutput, calls=%fused_computation.26 | convolution fusion | flops 1075838720 | bytes 11544064 | tf_op jit(solution)/shard_map/dot_general | solution.py:71
  79.1 1.0 copy.42
  80.1 7.0 %all-to-all-start.3 = ((bf16[128,16,128]{2,1,0:T(8,128)(2,1)}), bf16[128,16,128]{2,1,0:T(8,128)(2,1)S(1)}, u32[]{:S(2)}, u32[]{:S(2)}) async-start(bf16[128,16,128]{2,1,0:T(8,128)(2,1)} %bitcast.16), calls=%async_computation.3 | async-start | bytes 1048576 | tf_op jit(solution)/shard_map/all_to_all | solution.py:108
  87.2 4.9 %fusion.1 = bf16[2048,128]{0,1:T(8,128)(2,1)S(1)} fusion(bf16[2048,2048]{1,0:T(8,128)(2,1)} %param.11, f32[2048,128]{0,1:T(8,128)S(1)} %copy.36, f32[128]{0:T(128)S(1)} %fusion.14, f32[2048]{0:T(1024)S(1)} %copy-done, f32[128]{0:T(128)S(1)} %get-tuple-element.16), kind=kOutput, calls=%fused_computation.3 | convolution fusion | flops 1076625408 | bytes 9970688 | tf_op jit(solution)/shard_map/dot_general | solution.py:63
  93.0 14.1 %all-to-all-done.3 = bf16[128,16,128]{2,1,0:T(8,128)(2,1)S(1)} async-done(((bf16[128,16,128]{2,1,0:T(8,128)(2,1)}), bf16[128,16,128]{2,1,0:T(8,128)(2,1)S(1)}, u32[]{:S(2)}, u32[]{:S(2)}) %all-to-all-start.3) | async-done | bytes 524320 | tf_op jit(solution)/shard_map/all_to_all | solution.py:108
  107.1 6.8 %all-to-all-start.1 = ((bf16[128,16,128]{2,1,0:T(8,128)(2,1)}), bf16[128,16,128]{2,1,0:T(8,128)(2,1)S(1)}, u32[]{:S(2)}, u32[]{:S(2)}) async-start(bf16[128,16,128]{2,1,0:T(8,128)(2,1)} %bitcast.11), calls=%async_computation.1 | async-start | bytes 1048576 | tf_op jit(solution)/shard_map/all_to_all | solution.py:103
  114.4 1.3 collective-permute-start.2
  115.7 4.0 %collective-permute-start.3 = (bf16[16,1,1024]{2,1,0:T(2,128)(2,1)S(1)}, bf16[16,1,1024]{2,1,0:T(2,128)(2,1)S(1)}, u32[]{:S(2)}, u32[]{:S(2)}) collective-permute-start(bf16[16,1,1024]{2,1,0:T(2,128)(2,1)S(1)} %get-tuple-element.6), channel_id=1, source_target_pairs={{0,1},{2,3},{4,5},{6,7},{8,9},{10,11},{12,13},{14,15},{16,17},{18,... | collective-permute-start | bytes 98312 | tf_op jit(solution)/shard_map/ppermute | solution.py:16
  119.7 14.2 %all-to-all-done.1 = bf16[128,16,128]{2,1,0:T(8,128)(2,1)S(1)} async-done(((bf16[128,16,128]{2,1,0:T(8,128)(2,1)}), bf16[128,16,128]{2,1,0:T(8,128)(2,1)S(1)}, u32[]{:S(2)}, u32[]{:S(2)}) %all-to-all-start.1) | async-done | bytes 524320 | tf_op jit(solution)/shard_map/all_to_all | solution.py:103
  134.0 1.0 reshape.91
  135.1 2.5 %fusion.11 = bf16[16,16,1024]{2,1,0:T(8,128)(2,1)} fusion(bf16[16,16,1024]{2,1,0:T(8,128)(2,1)S(1)} %reshape.92, bf16[16,1,1024]{2,1,0:T(2,128)(2,1)S(1)} %collective-permute-done.3, bf16[16,1,1024]{2,1,0:T(2,128)(2,1)S(1)} %collective-permute-done.2, f32[16]{0:T(128)S(1)} %get-tuple-element.13, f32[16]{0:T(128)S(1)} %get-tuple-element.14, ...), kind=kLoop, calls=%fused_computation.21 | loop fusion | flops 7077888 | bytes 1116400 | tf_op jit(solution)/shard_map/convert_element_type | solution.py:112
  (26 shorter events, 5.8 us)
Async XLA Ops:
  0.6 71.1 %copy-start = (f32[2048]{0:T(1024)S(1)}, f32[2048]{0:T(1024)}, u32[]{:S(2)}) copy-start(f32[2048]{0:T(1024)} %param.12) | copy-start | bytes 24580
  3.0 36.3 %all-to-all-start.2 = ((bf16[16,128,128]{2,0,1:T(8,128)(2,1)}), bf16[16,128,128]{2,0,1:T(8,128)(2,1)S(1)}, u32[]{:S(2)}, u32[]{:S(2)}) async-start(bf16[16,128,128]{2,0,1:T(8,128)(2,1)} %copy.39), calls=%async_computation.2 | async-start | bytes 1048576 | tf_op jit(solution)/shard_map/all_to_all | solution.py:104
  20.6 5.2 %collective-permute-start = (bf16[16,1,1024]{2,1,0:T(2,128)(2,1)S(1)}, bf16[16,1,1024]{2,1,0:T(2,128)(2,1)S(1)}, u32[]{:S(2)}, u32[]{:S(2)}) collective-permute-start(bf16[16,1,1024]{2,1,0:T(2,128)(2,1)S(1)} %get-tuple-element.7), channel_id=1, source_target_pairs={{0,1},{2,3},{4,5},{6,7},{8,9},{10,11},{12,13},{14,15},{16,17},{18,... | collective-permute-start | bytes 98312 | tf_op jit(solution)/shard_map/ppermute | solution.py:16
  22.9 5.7 %collective-permute-start.1 = (bf16[16,1,1024]{2,1,0:T(2,128)(2,1)S(1)}, bf16[16,1,1024]{2,1,0:T(2,128)(2,1)S(1)}, u32[]{:S(2)}, u32[]{:S(2)}) collective-permute-start(bf16[16,1,1024]{2,1,0:T(2,128)(2,1)S(1)} %get-tuple-element.8), channel_id=1, source_target_pairs={{1,0},{3,2},{5,4},{7,6},{9,8},{11,10},{13,12},{15,14},{17,16},{19,... | collective-permute-start | bytes 98312 | tf_op jit(solution)/shard_map/ppermute | solution.py:17
  39.4 31.5 %all-to-all-start = ((bf16[16,128,128]{2,0,1:T(8,128)(2,1)}), bf16[16,128,128]{2,0,1:T(8,128)(2,1)S(1)}, u32[]{:S(2)}, u32[]{:S(2)}) async-start(bf16[16,128,128]{2,0,1:T(8,128)(2,1)} %copy.34), calls=%async_computation | async-start | bytes 1048576 | tf_op jit(solution)/shard_map/all_to_all | solution.py:101
  71.7 6.6 %copy-start.2 = (s32[1,128]{1,0:T(1,128)S(1)}, s32[1,128]{1,0:T(1,128)}, u32[]{:S(2)}) copy-start(s32[1,128]{1,0:T(1,128)} %param.17) | copy-start | bytes 1540
  71.7 6.6 %copy-start.3 = (f32[1,128]{1,0:T(1,128)S(1)}, f32[1,128]{1,0:T(1,128)}, u32[]{:S(2)}) copy-start(f32[1,128]{1,0:T(1,128)} %param.16) | copy-start | bytes 1540
  71.7 7.1 %copy-start.1 = (f32[2048]{0:T(1024)S(1)}, f32[2048]{0:T(1024)}, u32[]{:S(2)}) copy-start(f32[2048]{0:T(1024)} %param.13) | copy-start | bytes 24580
  80.1 27.0 %all-to-all-start.3 = ((bf16[128,16,128]{2,1,0:T(8,128)(2,1)}), bf16[128,16,128]{2,1,0:T(8,128)(2,1)S(1)}, u32[]{:S(2)}, u32[]{:S(2)}) async-start(bf16[128,16,128]{2,1,0:T(8,128)(2,1)} %bitcast.16), calls=%async_computation.3 | async-start | bytes 1048576 | tf_op jit(solution)/shard_map/all_to_all | solution.py:108
  107.1 26.8 %all-to-all-start.1 = ((bf16[128,16,128]{2,1,0:T(8,128)(2,1)}), bf16[128,16,128]{2,1,0:T(8,128)(2,1)S(1)}, u32[]{:S(2)}, u32[]{:S(2)}) async-start(bf16[128,16,128]{2,1,0:T(8,128)(2,1)} %bitcast.11), calls=%async_computation.1 | async-start | bytes 1048576 | tf_op jit(solution)/shard_map/all_to_all | solution.py:103
  114.4 20.6 %collective-permute-start.2 = (bf16[16,1,1024]{2,1,0:T(2,128)(2,1)S(1)}, bf16[16,1,1024]{2,1,0:T(2,128)(2,1)S(1)}, u32[]{:S(2)}, u32[]{:S(2)}) collective-permute-start(bf16[16,1,1024]{2,1,0:T(2,128)(2,1)S(1)} %get-tuple-element.5), channel_id=1, source_target_pairs={{1,0},{3,2},{5,4},{7,6},{9,8},{11,10},{13,12},{15,14},{17,16},{19,... | collective-permute-start | bytes 98312 | tf_op jit(solution)/shard_map/ppermute | solution.py:17
  115.7 19.3 %collective-permute-start.3 = (bf16[16,1,1024]{2,1,0:T(2,128)(2,1)S(1)}, bf16[16,1,1024]{2,1,0:T(2,128)(2,1)S(1)}, u32[]{:S(2)}, u32[]{:S(2)}) collective-permute-start(bf16[16,1,1024]{2,1,0:T(2,128)(2,1)S(1)} %get-tuple-element.6), channel_id=1, source_target_pairs={{0,1},{2,3},{4,5},{6,7},{8,9},{10,11},{12,13},{14,15},{16,17},{18,... | collective-permute-start | bytes 98312 | tf_op jit(solution)/shard_map/ppermute | solution.py:16
where the time goes:
time: 138 us
  waiting for transfers between devices  53.5 us (39%)
  starting transfers between devices  50.7 us (37%)
  local copies, waits for them, and re-layouts  11.5 us (8%)
  matrix products  11.4 us (8%)
  other arithmetic  9.58 us (7%)
    all_to_all x1, waiting for transfers between devices, body(): lax.all_to_all(flat_passed, 'vert', split_axis=1, concat_axis=0, tiled=True)  18.2 us
    all_to_all x1, starting transfers between devices, body(): lax.all_to_all(flat_cot, 'vert', split_axis=1, concat_axis=0, tiled=True)  16.4 us
    all_to_all x1, waiting for transfers between devices, body(): lax.all_to_all(advanced, 'vert', split_axis=0, concat_axis=1, tiled=True)  14.2 us
    all_to_all x1, waiting for transfers between devices, body(): lax.all_to_all(adjoint_g, 'vert', split_axis=0, concat_axis=1, tiled=True)  14.1 us
    all_to_all x1, starting transfers between devices, body(): lax.all_to_all(flat_passed, 'vert', split_axis=1, concat_axis=0, tiled=True)  11.6 us
    all_to_all x1, starting transfers between devices, body(): lax.all_to_all(adjoint_g, 'vert', split_axis=0, concat_axis=1, tiled=True)  7.01 us
    all_to_all x1, starting transfers between devices, body(): lax.all_to_all(advanced, 'vert', split_axis=0, concat_axis=1, tiled=True)  6.83 us
    dot_general x1, matrix products, collide_adjoint(): jnp.dot(collision, adjoint_in, preferred_element_type=jnp.float32)  6.55 us
  transfers between devices with their start and end apart: 8, of which 5 were waited for; matrix products, arithmetic and copies ran while one was open for 13% of the time, Pallas kernels for 0%

commit v1 on v0

v1 whole, which is shorter than its diff:
```python
import jax
import jax.numpy as jnp
from jax import lax
from jax.experimental import pallas as pl
from jax.experimental.pallas import tpu as pltpu
from jax.sharding import PartitionSpec as P

MESH = pl.DeviceIdType.MESH
F32 = jnp.float32
BF16 = jnp.bfloat16
NZ = 32
LANES = 128
VL = 16
SLAB = 16
YB = 8
NB = SLAB * YB
TILE = 256
PER = TILE // VL
NT = 2048 // TILE


def column(row, n):
    r = lax.broadcasted_iota(jnp.int32, (n, n), 0)
    c = lax.broadcasted_iota(jnp.int32, (n, n), 1)
    one = jnp.sum(jnp.where(r == c, jnp.broadcast_to(row, (n, n)), 0.0), axis=1, keepdims=True)
    return jnp.broadcast_to(one, (n, LANES))


def step_kernel(
    state_ref, cot_ref, coll_ref, shape_ref, flux_ref, cour_ref, bits_ref, acc_ref, flag_ref,
    adv_ref, prev_ref, sens_ref,
    svm, cvm, cmat, turn, halo_s, halo_g,
    cot_s, pas_s, adj_s, adv_s, cot_r, pas_r, adv_r,
    ws, wf, hbuf, xbuf, rt, coef, masks,
    load_sem, send_sem, recv_sem, face_ss, face_rs,
):
    me = lax.axis_index("vert")
    sa = lax.axis_index("sa")
    my_tile, my_pos = me // PER, me % PER

    loads = [
        pltpu.make_async_copy(cot_ref, cvm, load_sem.at[0]),
        pltpu.make_async_copy(state_ref, svm, load_sem.at[1]),
        pltpu.make_async_copy(coll_ref, cmat, load_sem.at[2]),
    ]
    for c in loads:
        c.start()

    def peer(tile, pos):
        return ((my_tile + tile) % NT) * PER + (my_pos + pos) % PER

    barrier = pltpu.get_barrier_semaphore()
    pl.semaphore_signal(barrier, inc=1, device_id={"sa": 1 - sa}, device_id_type=MESH)

    def greet(k, _):
        pl.semaphore_signal(
            barrier, inc=1, device_id={"vert": peer(k // PER, k % PER)}, device_id_type=MESH
        )
        return 0

    lax.fori_loop(1, NB, greet, 0)

    for d in range(3):
        coef[d] = column(cour_ref[d : d + 1, :], VL)
        masks[d] = column(bits_ref[d : d + 1, :].astype(F32), VL)
    zero_plane = jnp.zeros((YB, VL, LANES), BF16)
    lone = sa * (NB + YB)
    halo_s[pl.ds(lone, YB)] = zero_plane
    halo_g[pl.ds(lone, YB)] = zero_plane

    def to_blocks(src, dst, base):
        def rows_in(v, _):
            plane = src[v].astype(F32)
            for j in range(YB):
                turn[j, pl.ds(v, SLAB, stride=VL), :] = plane[:, j * LANES : (j + 1) * LANES]
            return 0

        lax.fori_loop(0, VL, rows_in, 0, unroll=4)

        def planes_out(x, _):
            for j in range(YB):
                part = turn[j, pl.ds(pl.multiple_of(x * VL, VL), VL), :]
                dst[base + x * YB + j] = part.astype(BF16)
            return 0

        lax.fori_loop(0, SLAB, planes_out, 0, unroll=2)

    def send(src, src_base, dst, dst_base, phase, tile, pos):
        d = peer(tile, pos)
        pltpu.make_async_remote_copy(
            src_ref=src.at[src_base + d],
            dst_ref=dst.at[dst_base + me],
            send_sem=send_sem.at[phase],
            recv_sem=recv_sem.at[phase],
            device_id={"vert": d},
            device_id_type=MESH,
        ).start()

    def send_tile(src, src_base, dst, dst_base, phase, tile):
        def one(pos, _):
            send(src, src_base, dst, dst_base, phase, tile, pos)
            return 0

        lax.fori_loop(1 - jnp.minimum(tile, 1), PER, one, 0)

    def send_all(src, src_base, dst, dst_base, phase):
        def one(k, _):
            send(src, src_base, dst, dst_base, phase, k // PER, k % PER)
            return 0

        lax.fori_loop(1, NB, one, 0)

    def wait_blocks(ref, sem):
        part = ref.at[pl.ds(0, NB - 1)]
        pltpu.make_async_copy(part, part, sem).wait()

    def face(buf, k):
        return pltpu.make_async_remote_copy(
            src_ref=buf.at[pl.ds(YB + (NB - YB) * (1 - sa), YB)],
            dst_ref=buf.at[pl.ds((NB + YB) * sa, YB)],
            send_sem=face_ss.at[k],
            recv_sem=face_rs.at[k],
            device_id={"sa": 1 - sa},
            device_id_type=MESH,
        )

    lane = lax.broadcasted_iota(jnp.int32, (VL, LANES), 1)
    z_at = lane % NZ

    def transport(buf, forward, emit):
        def plane(x, _):
            base = x * YB
            mid = [buf[base + YB + j].astype(F32) for j in range(YB)]
            up32 = [pltpu.roll(m, NZ, 1) for m in mid]
            dn32 = [pltpu.roll(m, LANES - NZ, 1) for m in mid]
            zero = jnp.zeros((VL, LANES), F32)
            for j in range(YB):
                m = mid[j]
                minus = (
                    buf[base + j].astype(F32),
                    jnp.where(lane < NZ, up32[j - 1] if j else zero, up32[j]),
                    jnp.where(z_at != 0, pltpu.roll(m, 1, 1), 0.0),
                )
                plus = (
                    buf[base + 2 * YB + j].astype(F32),
                    jnp.where(lane >= LANES - NZ, dn32[j + 1] if j < YB - 1 else zero, dn32[j]),
                    jnp.where(z_at != NZ - 1, pltpu.roll(m, LANES - 1, 1), 0.0),
                )
                res = m
                for d in range(3):
                    up = masks[d] == 1.0
                    donor = jnp.where(up, minus[d], plus[d]) if forward else jnp.where(up, plus[d], minus[d])
                    res = res - coef[d] * (m - donor)
                emit(x, j, res)
            return 0

        lax.fori_loop(0, SLAB, plane, 0)

    def out_rows(dst):
        def one(v, _):
            for j in range(YB):
                rows = turn[j, pl.ds(pl.multiple_of(v * SLAB, SLAB), SLAB), :]
                dst[v, :, j * LANES : (j + 1) * LANES] = rows.astype(BF16)
            return 0

        lax.fori_loop(0, VL, one, 0, unroll=2)

    loads[0].wait()
    to_blocks(cvm, cot_s, 0)
    loads[1].wait()
    to_blocks(svm, halo_s, YB)

    pl.semaphore_wait(barrier, NB)
    face_s = face(halo_s, 0)
    face_s.start()
    send_all(cot_s, 0, cot_r, 0, 0)
    cot_r[me] = cot_s[me]

    face_s.wait()

    def emit_passed(x, j, res):
        pas_s[x * YB + j] = res.astype(BF16)

    transport(halo_s, True, emit_passed)
    send_all(pas_s, 0, pas_r, 0, 1)
    pas_r[me] = pas_s[me]

    def spread(g, _):
        rows = pl.ds(pl.multiple_of(g * LANES, LANES), LANES)
        ws[rows, :] = jnp.broadcast_to(shape_ref[pl.ds(g, 1), :], (LANES, LANES)).T
        wf[rows, :] = jnp.broadcast_to(flux_ref[pl.ds(g, 1), :], (LANES, LANES)).T
        return 0

    lax.fori_loop(0, 2048 // LANES, spread, 0)
    flags = flag_ref[...].astype(F32)
    gain = acc_ref[...] * flags

    def tile_rows(t):
        return pl.ds(pl.multiple_of(t * TILE, TILE), TILE)

    def tile_blocks(t):
        return pl.ds(pl.multiple_of(t * PER, PER), PER)

    def fold(a):
        return jnp.sum(a.reshape(TILE // 8, 8, LANES), axis=0)

    loads[2].wait()
    wait_blocks(cot_r, recv_sem.at[0])
    cot_all = cot_r.reshape(2048, LANES)

    def adjoint_tile(t, total):
        rows = tile_rows(t)
        h = jnp.dot(cmat[rows, :], cot_all[...], preferred_element_type=F32)
        h = cot_all[rows, :].astype(F32) + h
        hbuf[rows, :] = h
        return total + fold(ws[rows, :] * h)

    total = lax.fori_loop(0, NT, adjoint_tile, jnp.zeros((8, LANES), F32))
    weighted = jnp.sum(total, axis=0, keepdims=True)

    def adjoint_out(k, _):
        t = (my_tile + k) % NT
        rows = tile_rows(t)
        h = hbuf[rows, :]
        g = h + gain * (wf[rows, :] * weighted - h)
        adj_s[tile_blocks(t)] = g.astype(BF16).reshape(PER, VL, LANES)
        return 0

    lax.fori_loop(0, NT, adjoint_out, 0)
    send_all(adj_s, 0, halo_g, YB, 2)
    halo_g[YB + me] = adj_s[me]

    wait_blocks(pas_r, recv_sem.at[1])
    pas_all = pas_r.reshape(2048, LANES)

    def density_tile(t, total):
        rows = tile_rows(t)
        return total + fold(wf[rows, :] * pas_all[rows, :].astype(F32))

    total = lax.fori_loop(0, NT, density_tile, jnp.zeros((8, LANES), F32))
    density = jnp.sum(total, axis=0, keepdims=True)

    def relax_block(g, total):
        rows = pl.ds(pl.multiple_of(g * LANES, LANES), LANES)
        moved = pas_all[rows, :].astype(F32)
        target = ws[rows, :] * density - moved
        relaxed = moved + gain * target
        xbuf[rows, :] = relaxed
        rt[:, rows] = relaxed.T.astype(BF16)
        return total + jnp.sum((hbuf[rows, :] * target).reshape(LANES // 8, 8, LANES), axis=0)

    total = lax.fori_loop(0, 2048 // LANES, relax_block, jnp.zeros((8, LANES), F32))
    sens_ref[...] = flags * jnp.sum(total, axis=0, keepdims=True)

    def forward_tile(k, _):
        t = (my_tile + k) % NT
        rows = tile_rows(t)
        mixed = jnp.dot(rt[...], cmat[:, rows], preferred_element_type=F32)
        adv = xbuf[rows, :] + mixed.T
        adv_s[tile_blocks(t)] = adv.astype(BF16).reshape(PER, VL, LANES)

        @pl.when(k > 0)
        def _():
            send_tile(adv_s, 0, adv_r, 0, 3, k - 1)

        return 0

    lax.fori_loop(0, NT, forward_tile, 0)
    send_tile(adv_s, 0, adv_r, 0, 3, NT - 1)
    adv_r[me] = adv_s[me]

    wait_blocks(halo_g, recv_sem.at[2])
    face_g = face(halo_g, 1)
    face_g.start()
    face_g.wait()

    def emit_previous(x, j, res):
        turn[j, pl.ds(x, VL, stride=SLAB), :] = res

    transport(halo_g, False, emit_previous)
    out_rows(prev_ref)

    wait_blocks(adv_r, recv_sem.at[3])

    def unpack(x, _):
        for j in range(YB):
            turn[j, pl.ds(x, VL, stride=SLAB), :] = adv_r[x * YB + j].astype(F32)
        return 0

    lax.fori_loop(0, SLAB, unpack, 0, unroll=2)
    out_rows(adv_ref)

    for phase, buf in enumerate((cot_s, pas_s, adj_s, adv_s)):
        wait_blocks(buf, send_sem.at[phase])


def body(state, cotangent, collision, wall_shape, flux_weight, courant, upwind_bits, accommodation, wall_flags):
    vm = pl.BlockSpec(memory_space=pltpu.VMEM)
    hb = pl.BlockSpec(memory_space=pl.ANY)
    blocks = pltpu.VMEM((NB, VL, LANES), BF16)
    full = pltpu.VMEM((2048, LANES), F32)
    return pl.pallas_call(
        step_kernel,
        name="step",
        out_shape=(
            jax.ShapeDtypeStruct(state.shape, BF16),
            jax.ShapeDtypeStruct(state.shape, BF16),
            jax.ShapeDtypeStruct(accommodation.shape, F32),
        ),
        in_specs=[hb, hb, hb] + [vm] * 6,
        out_specs=(vm, vm, vm),
        scratch_shapes=[
            pltpu.VMEM(state.shape, BF16),
            pltpu.VMEM(state.shape, BF16),
            pltpu.VMEM(collision.shape, BF16),
            pltpu.VMEM((YB, VL * SLAB, LANES), F32),
            pltpu.VMEM((NB + 2 * YB, VL, LANES), BF16),
            pltpu.VMEM((NB + 2 * YB, VL, LANES), BF16),
            *[blocks] * 7,
            *[full] * 4,
            pltpu.VMEM((LANES, 2048), BF16),
            pltpu.VMEM((3, VL, LANES), F32),
            pltpu.VMEM((3, VL, LANES), F32),
            pltpu.SemaphoreType.DMA((3,)),
            pltpu.SemaphoreType.DMA((4,)),
            pltpu.SemaphoreType.DMA((4,)),
            pltpu.SemaphoreType.DMA((2,)),
            pltpu.SemaphoreType.DMA((2,)),
        ],
        compiler_params=pltpu.CompilerParams(
            collective_id=0, has_side_effects=True, vmem_limit_bytes=56 * 1024 * 1024
        ),
    )(
        state, cotangent, collision, wall_shape.reshape(16, LANES), flux_weight.reshape(16, LANES),
        courant, upwind_bits, accommodation, wall_flags,
    )


def solution(mesh):
    return jax.shard_map(
        body,
        mesh=mesh,
        in_specs=(
            P("vert", "sa", None),
            P("vert", "sa", None),
            P(),
            P(),
            P(),
            P(None, "vert"),
            P(None, "vert"),
            P(("vert", "sa"), None),
            P(("vert", "sa"), None),
        ),
        out_specs=(P("vert", "sa", None), P("vert", "sa", None), P(("vert", "sa"), None)),
        check_vma=False,
    )
```

time: 138 us -> 70.6 us (0.51)
  Pallas kernels: 0 us -> 64.5 us
  waiting for transfers between devices: 53.5 us -> 0 us
  starting transfers between devices: 50.7 us -> 0 us
  matrix products: 11.4 us -> 0 us
  other arithmetic: 9.58 us -> 0 us
  local copies, waits for them, and re-layouts: 11.5 us -> 4.87 us
    pallas_call x0 -> x1, Pallas kernels: none -> 64.5 us  [body(): pl.pallas_call(step_kernel, name='step', out_shape=(jax.ShapeDtypeStruct(...]
    all_to_all x4 -> x0, waiting for transfers between devices: 50.7 us -> none  [the longest x1 18.2 us: body(): lax.all_to_all(flat_passed, 'vert', split_axis=1, concat_axis=0, tiled=True)]
    all_to_all x4 -> x0, starting transfers between devices: 41.8 us -> none  [the longest x1 16.4 us: body(): lax.all_to_all(flat_cot, 'vert', split_axis=1, concat_axis=0, tiled=True)]
    dot_general x2 -> x0, matrix products: 11.4 us -> none  [the longest x1 6.55 us: collide_adjoint(): jnp.dot(collision, adjoint_in, preferred_element_type=jnp.float32)]
    ppermute x4 -> x0, starting transfers between devices: 8.88 us -> none  [the longest x2 6.29 us: padded_2(): before = lax.ppermute(last, axis, up)]
    convert_element_type x4 -> x0, other arithmetic: 7.91 us -> none  [the longest x1 5.08 us: body(): transport(padded, courant, upwind_bits, NZ, True).astype(jnp.bfloat16)]
    all_to_all x7 -> x0, local copies, waits for them, and re-layouts: 5.05 us -> none  [the longest x3 3.42 us: body(): lax.all_to_all(flat_cot, 'vert', split_axis=1, concat_axis=0, tiled=True)]
    unnamed x8 -> x3, local copies, waits for them, and re-layouts: 0.02 us -> 4.87 us
  transfers between devices with their start and end apart: 8 -> 0, of which waited for: 5 -> 0; matrix products, arithmetic and copies ran while one was open for 13% -> 0% of each run, Pallas kernels for 0% -> 0%
where the time goes in v1:
time: 70.6 us; the launch traced here: 70.1 us
  Pallas kernels  64.5 us (91%)
  local copies, waits for them, and re-layouts  4.87 us (7%)
    pallas_call x1, Pallas kernels, body(): pl.pallas_call(step_kernel, name='step', out_shape=(jax.ShapeDtypeStruct(...  64.5 us
    unnamed x3, local copies, waits for them, and re-layouts  4.87 us

profile of v1, /device:TPU:1, one launch (start us, length us, event | category | flops | bytes accessed | tf_op | source)
XLA Modules:
  0.0 70.1 jit_solution(1995991512153007220)
XLA Ops:
  0.6 64.5 %step.1 = (bf16[16,16,1024]{2,1,0:T(8,128)(2,1)}, bf16[16,16,1024]{2,1,0:T(8,128)(2,1)}, f32[1,128]{1,0:T(1,128)}) custom-call(bf16[16,16,1024]{2,1,0:T(8,128)(2,1)} %state_ref.1, bf16[16,16,1024]{2,1,0:T(8,128)(2,1)} %cot_ref.1, bf16[2048,2048]{1,0:T(8,128)(2,1)} %coll_ref.1, f32[16,128]{1,0:T(8,128)} %bitcast.2, f32[16,128]{1,0:T(8,128)} %bitcast.3, ...), custom_call_target="tpu_custom_call" | custom-call | tf_op jit(solution)/shard_map/step/pallas_call | solution.py:302
  65.2 1.9 %copy.15 = bf16[16,16,1024]{2,1,0:T(8,128)(2,1)} copy(bf16[16,16,1024]{2,1,0:T(8,128)(2,1)} %get-tuple-element.6) | data formatting | bytes 1048576
  67.1 1.9 %copy.16 = bf16[16,16,1024]{2,1,0:T(8,128)(2,1)} copy(bf16[16,16,1024]{2,1,0:T(8,128)(2,1)} %get-tuple-element.7) | data formatting | bytes 1048576
  68.9 1.1 %copy.17 = f32[1,128]{1,0:T(1,128)} copy(f32[1,128]{1,0:T(1,128)} %get-tuple-element.8) | data formatting | bytes 1024

commit v2 on v1

--- a/solution.py
+++ b/solution.py
@@ -17,6 +17,7 @@
 TILE = 256
 PER = TILE // VL
 NT = 2048 // TILE
+FAR_COLUMNS = ((1, 2), (1, 3), (1, 1), (1, 0), (0, 2), (0, 3), (0, 1), (0, 0))
 
 
 def column(row, n):
@@ -27,8 +28,9 @@
 
 
 def step_kernel(
-    state_ref, cot_ref, coll_ref, shape_ref, flux_ref, cour_ref, bits_ref, acc_ref, flag_ref,
+    state_ref, cot_ref, coll_ref, shape_hbm, flux_hbm, cour_hbm, bits_hbm, acc_hbm, flag_hbm,
     adv_ref, prev_ref, sens_ref,
+    shape_ref, flux_ref, cour_ref, bits_ref, acc_ref, flag_ref,
     svm, cvm, cmat, turn, halo_s, halo_g,
     cot_s, pas_s, adj_s, adv_s, cot_r, pas_r, adv_r,
     ws, wf, hbuf, xbuf, rt, coef, masks,
@@ -36,29 +38,50 @@
 ):
     me = lax.axis_index("vert")
     sa = lax.axis_index("sa")
-    my_tile, my_pos = me // PER, me % PER
+    my_y, my_x, my_z, my_core = me // 64, (me // PER) % 4, (me // 2) % 8, me % 2
+    my_column = [(my_y + dy) % 2 * 4 + (my_x + dx) % 4 for dy, dx in FAR_COLUMNS]
+    my_cores = [(my_core + 1) % 2, my_core]
+    near = [c * PER + core for c in my_column for core in my_cores]
 
     loads = [
         pltpu.make_async_copy(cot_ref, cvm, load_sem.at[0]),
         pltpu.make_async_copy(state_ref, svm, load_sem.at[1]),
         pltpu.make_async_copy(coll_ref, cmat, load_sem.at[2]),
     ]
+    small = (
+        (shape_hbm, shape_ref), (flux_hbm, flux_ref), (cour_hbm, cour_ref),
+        (bits_hbm, bits_ref), (acc_hbm, acc_ref), (flag_hbm, flag_ref),
+    )
+    loads += [pltpu.make_async_copy(src, dst, load_sem.at[3 + i]) for i, (src, dst) in enumerate(small)]
     for c in loads:
         c.start()
 
-    def peer(tile, pos):
-        return ((my_tile + tile) % NT) * PER + (my_pos + pos) % PER
-
     barrier = pltpu.get_barrier_semaphore()
+
+    def far_z(i):
+        return (my_z + 4 + i // 2 - (i % 2) * i) % 8
+
+    def each_peer(visit):
+        def place(i, _):
+            z2 = far_z(i) * 2
+            for n in near[:-1]:
+                visit(z2 + n)
+
+            @pl.when(i < 7)
+            def _():
+                visit(z2 + near[-1])
+
+            return 0
+
+        lax.fori_loop(0, 8, place, 0)
+
+    def greet(d):
+        pl.semaphore_signal(barrier, inc=1, device_id={"vert": d}, device_id_type=MESH)
+
+    each_peer(greet)
     pl.semaphore_signal(barrier, inc=1, device_id={"sa": 1 - sa}, device_id_type=MESH)
-
-    def greet(k, _):
-        pl.semaphore_signal(
-            barrier, inc=1, device_id={"vert": peer(k // PER, k % PER)}, device_id_type=MESH
-        )
-        return 0
-
-    lax.fori_loop(1, NB, greet, 0)
+    for c in loads[3:]:
+        c.wait()
 
     for d in range(3):
         coef[d] = column(cour_ref[d : d + 1, :], VL)
@@ -85,8 +108,7 @@
 
         lax.fori_loop(0, SLAB, planes_out, 0, unroll=2)
 
-    def send(src, src_base, dst, dst_base, phase, tile, pos):
-        d = peer(tile, pos)
+    def send(src, src_base, dst, dst_base, phase, d):
         pltpu.make_async_remote_copy(
             src_ref=src.at[src_base + d],
             dst_ref=dst.at[dst_base + me],
@@ -96,19 +118,27 @@
             device_id_type=MESH,
         ).start()
 
-    def send_tile(src, src_base, dst, dst_base, phase, tile):
-        def one(pos, _):
-            send(src, src_base, dst, dst_base, phase, tile, pos)
-            return 0
-
-        lax.fori_loop(1 - jnp.minimum(tile, 1), PER, one, 0)
+    def column_of(k):
+        dx = 2 + k % 4 - (k % 4 // 2) * (2 * (k % 4) - 1)
+        return (my_y + 1 - k // 4) % 2 * 4 + (my_x + dx) % 4
+
+    def send_column(src, dst, phase, k):
+        first = column_of(k) * PER
+
+        def place(i, _):
+            z2 = far_z(i) * 2 + first
+            send(src, 0, dst, 0, phase, z2 + my_cores[0])
+
+            @pl.when(i + k < 14)
+            def _():
+                send(src, 0, dst, 0, phase, z2 + my_cores[1])
+
+            return 0
+
+        lax.fori_loop(0, 8, place, 0)
 
     def send_all(src, src_base, dst, dst_base, phase):
-        def one(k, _):
-            send(src, src_base, dst, dst_base, phase, k // PER, k % PER)
-            return 0
-
-        lax.fori_loop(1, NB, one, 0)
+        each_peer(lambda d: send(src, src_base, dst, dst_base, phase, d))
 
     def wait_blocks(ref, sem):
         part = ref.at[pl.ds(0, NB - 1)]
@@ -219,11 +249,10 @@
     weighted = jnp.sum(total, axis=0, keepdims=True)
 
     def adjoint_out(k, _):
-        t = (my_tile + k) % NT
-        rows = tile_rows(t)
+        rows = tile_rows(k)
         h = hbuf[rows, :]
         g = h + gain * (wf[rows, :] * weighted - h)
-        adj_s[tile_blocks(t)] = g.astype(BF16).reshape(PER, VL, LANES)
+        adj_s[tile_blocks(k)] = g.astype(BF16).reshape(PER, VL, LANES)
         return 0
 
     lax.fori_loop(0, NT, adjoint_out, 0)
@@ -253,7 +282,7 @@
     sens_ref[...] = flags * jnp.sum(total, axis=0, keepdims=True)
 
     def forward_tile(k, _):
-        t = (my_tile + k) % NT
+        t = column_of(k)
         rows = tile_rows(t)
         mixed = jnp.dot(rt[...], cmat[:, rows], preferred_element_type=F32)
         adv = xbuf[rows, :] + mixed.T
@@ -261,12 +290,12 @@
 
         @pl.when(k > 0)
         def _():
-            send_tile(adv_s, 0, adv_r, 0, 3, k - 1)
+            send_column(adv_s, adv_r, 3, k - 1)
 
         return 0
 
     lax.fori_loop(0, NT, forward_tile, 0)
-    send_tile(adv_s, 0, adv_r, 0, 3, NT - 1)
+    send_column(adv_s, adv_r, 3, NT - 1)
     adv_r[me] = adv_s[me]
 
     wait_blocks(halo_g, recv_sem.at[2])
@@ -294,12 +323,21 @@
         wait_blocks(buf, send_sem.at[phase])
 
 
+def write_kernel(a_ref, b_ref, c_ref, a_out, b_out, c_out, sems):
+    pairs = ((a_ref, a_out), (b_ref, b_out), (c_ref, c_out))
+    copies = [pltpu.make_async_copy(src, dst, sems.at[i]) for i, (src, dst) in enumerate(pairs)]
+    for c in copies:
+        c.start()
+    for c in copies:
+        c.wait()
+
+
 def body(state, cotangent, collision, wall_shape, flux_weight, courant, upwind_bits, accommodation, wall_flags):
     vm = pl.BlockSpec(memory_space=pltpu.VMEM)
-    hb = pl.BlockSpec(memory_space=pl.ANY)
+    hb = pl.BlockSpec(memory_space=pltpu.HBM)
     blocks = pltpu.VMEM((NB, VL, LANES), BF16)
     full = pltpu.VMEM((2048, LANES), F32)
-    return pl.pallas_call(
+    results = pl.pallas_call(
         step_kernel,
         name="step",
         out_shape=(
@@ -307,9 +345,15 @@
             jax.ShapeDtypeStruct(state.shape, BF16),
             jax.ShapeDtypeStruct(accommodation.shape, F32),
         ),
-        in_specs=[hb, hb, hb] + [vm] * 6,
+        in_specs=[hb] * 9,
         out_specs=(vm, vm, vm),
         scratch_shapes=[
+            pltpu.VMEM((16, LANES), F32),
+            pltpu.VMEM((16, LANES), F32),
+            pltpu.VMEM(courant.shape, F32),
+            pltpu.VMEM(upwind_bits.shape, jnp.int32),
+            pltpu.VMEM(accommodation.shape, F32),
+            pltpu.VMEM(wall_flags.shape, jnp.int32),
             pltpu.VMEM(state.shape, BF16),
             pltpu.VMEM(state.shape, BF16),
             pltpu.VMEM(collision.shape, BF16),
@@ -321,19 +365,28 @@
             pltpu.VMEM((LANES, 2048), BF16),
             pltpu.VMEM((3, VL, LANES), F32),
             pltpu.VMEM((3, VL, LANES), F32),
-            pltpu.SemaphoreType.DMA((3,)),
+            pltpu.SemaphoreType.DMA((9,)),
             pltpu.SemaphoreType.DMA((4,)),
             pltpu.SemaphoreType.DMA((4,)),
             pltpu.SemaphoreType.DMA((2,)),
             pltpu.SemaphoreType.DMA((2,)),
         ],
         compiler_params=pltpu.CompilerParams(
-            collective_id=0, has_side_effects=True, vmem_limit_bytes=56 * 1024 * 1024
+            collective_id=0, has_side_effects=True, vmem_limit_bytes=55312384
         ),
     )(
         state, cotangent, collision, wall_shape.reshape(16, LANES), flux_weight.reshape(16, LANES),
         courant, upwind_bits, accommodation, wall_flags,
     )
+    return pl.pallas_call(
+        write_kernel,
+        name="write",
+        out_shape=tuple(jax.ShapeDtypeStruct(r.shape, r.dtype) for r in results),
+        in_specs=[vm] * 3,
+        out_specs=(hb, hb, hb),
+        scratch_shapes=[pltpu.SemaphoreType.DMA((3,))],
+        compiler_params=pltpu.CompilerParams(vmem_limit_bytes=1024 * 1024),
+    )(*results)
 
 
 def solution(mesh):

time: 70.6 us -> 67.4 us (0.955)
  Pallas kernels: 64.5 us -> 62.4 us
  local copies, waits for them, and re-layouts: 4.87 us -> 4.06 us
    pallas_call x1, Pallas kernels: 64.5 us -> 61.4 us  [body(): pl.pallas_call(step_kernel, name='step', out_shape=(jax.ShapeDtypeStruct(...]
    pallas_call x0 -> x1, Pallas kernels: none -> 1 us  [body(): pl.pallas_call(write_kernel, name='write', out_shape=tuple((jax.ShapeDtyp...]
    unnamed x3 -> x12, local copies, waits for them, and re-layouts: 4.87 us -> 4.06 us
where the time goes in v2:
time: 67.4 us; the launch traced here: 67.1 us
  Pallas kernels  62.4 us (93%)
  local copies, waits for them, and re-layouts  4.06 us (6%)
    pallas_call x1, Pallas kernels, body(): pl.pallas_call(step_kernel, name='step', out_shape=(jax.ShapeDtypeStruct(...  61.4 us
    unnamed x12, local copies, waits for them, and re-layouts  4.06 us

profile of v2, /device:TPU:1, one launch (start us, length us, event | category | flops | bytes accessed | tf_op | source)
XLA Modules:
  0.0 67.1 jit_solution(13632036159886472083)
XLA Ops:
  0.6 0.0 copy-start
  0.6 0.7 %copy-done = f32[2048]{0:T(1024)S(1)} copy-done((f32[2048]{0:T(1024)S(1)}, f32[2048]{0:T(1024)}, u32[]{:S(2)}) %copy-start) | copy-done | bytes 8216
  1.3 0.0 copy-start.1
  1.3 0.7 %copy-done.1 = f32[2048]{0:T(1024)S(1)} copy-done((f32[2048]{0:T(1024)S(1)}, f32[2048]{0:T(1024)}, u32[]{:S(2)}) %copy-start.1) | copy-done | bytes 8216
  2.0 0.0 copy-start.2
  2.0 0.7 %copy-done.2 = f32[3,16]{1,0:T(4,128)S(1)} copy-done((f32[3,16]{1,0:T(4,128)S(1)}, f32[3,16]{1,0:T(4,128)}, u32[]{:S(2)}) %copy-start.2) | copy-done | bytes 216
  2.7 0.0 copy-start.3
  2.7 0.7 %copy-done.3 = s32[3,16]{1,0:T(4,128)S(1)} copy-done((s32[3,16]{1,0:T(4,128)S(1)}, s32[3,16]{1,0:T(4,128)}, u32[]{:S(2)}) %copy-start.3) | copy-done | bytes 216
  3.4 0.0 copy-start.4
  3.4 0.7 copy-done.4
  4.0 0.0 copy-start.5
  4.1 0.7 copy-done.5
  4.7 61.4 %step.1 = (bf16[16,16,1024]{2,1,0:T(8,128)(2,1)S(1)}, bf16[16,16,1024]{2,1,0:T(8,128)(2,1)S(1)}, f32[1,128]{1,0:T(1,128)S(1)}) custom-call(bf16[16,16,1024]{2,1,0:T(8,128)(2,1)} %state_ref.1, bf16[16,16,1024]{2,1,0:T(8,128)(2,1)} %cot_ref.1, bf16[2048,2048]{1,0:T(8,128)(2,1)} %coll_ref.1, f32[16,128]{1,0:T(8,128)S(1)} %bitcast.2, f32[16,128]{1,0:T(8,128)S(1)} %bitcast.3, ...), custom_call_target="tpu_custom_call" | custom-call | tf_op jit(solution)/shard_map/step/pallas_call | solution.py:340
  66.1 1.0 %write.1 = (bf16[16,16,1024]{2,1,0:T(8,128)(2,1)}, bf16[16,16,1024]{2,1,0:T(8,128)(2,1)}, f32[1,128]{1,0:T(1,128)}) custom-call(bf16[16,16,1024]{2,1,0:T(8,128)(2,1)S(1)} %get-tuple-element.6.a_ref, bf16[16,16,1024]{2,1,0:T(8,128)(2,1)S(1)} %get-tuple-element.7.b_ref, f32[1,128]{1,0:T(1,128)S(1)} %get-tuple-element.8.c_ref), custom_call_target="tpu_custom_call" | custom-call | tf_op jit(solution)/shard_map/write/pallas_call | solution.py:381
Async XLA Ops:
  0.6 0.7 %copy-start = (f32[2048]{0:T(1024)S(1)}, f32[2048]{0:T(1024)}, u32[]{:S(2)}) copy-start(f32[2048]{0:T(1024)} %param.12) | copy-start | bytes 24580
  1.3 0.7 %copy-start.1 = (f32[2048]{0:T(1024)S(1)}, f32[2048]{0:T(1024)}, u32[]{:S(2)}) copy-start(f32[2048]{0:T(1024)} %param.13) | copy-start | bytes 24580
  2.0 0.7 %copy-start.2 = (f32[3,16]{1,0:T(4,128)S(1)}, f32[3,16]{1,0:T(4,128)}, u32[]{:S(2)}) copy-start(f32[3,16]{1,0:T(4,128)} %cour_hbm.1) | copy-start | bytes 580
  2.7 0.7 %copy-start.3 = (s32[3,16]{1,0:T(4,128)S(1)}, s32[3,16]{1,0:T(4,128)}, u32[]{:S(2)}) copy-start(s32[3,16]{1,0:T(4,128)} %bits_hbm.1) | copy-start | bytes 580
  3.4 0.7 copy-start.4
  4.0 0.7 copy-start.5

commit v3 on v2

--- a/solution.py
+++ b/solution.py
@@ -372,11 +372,16 @@
             pltpu.SemaphoreType.DMA((2,)),
         ],
         compiler_params=pltpu.CompilerParams(
-            collective_id=0, has_side_effects=True, vmem_limit_bytes=55312384
+            collective_id=0, has_side_effects=True, vmem_limit_bytes=32 * 1024 * 1024
         ),
     )(
-        state, cotangent, collision, wall_shape.reshape(16, LANES), flux_weight.reshape(16, LANES),
-        courant, upwind_bits, accommodation, wall_flags,
+        *[
+            pltpu.with_memory_space_constraint(a, pltpu.HBM)
+            for a in (
+                state, cotangent, collision, wall_shape.reshape(16, LANES), flux_weight.reshape(16, LANES),
+                courant, upwind_bits, accommodation, wall_flags,
+            )
+        ]
     )
     return pl.pallas_call(
         write_kernel,

time: 67.4 us -> 63.3 us (0.939)
  local copies, waits for them, and re-layouts: 4.06 us -> 0 us
    unnamed x12 -> x0, local copies, waits for them, and re-layouts: 4.06 us -> none
where the time goes in v3:
time: 63.3 us; the launch traced here: 63.2 us
  Pallas kernels  62.6 us (99%)
  between operations  0.64 us (1%)
    pallas_call x1, Pallas kernels, body(): pl.pallas_call(step_kernel, name='step', out_shape=(jax.ShapeDtypeStruct(...  61.6 us

profile of v3, /device:TPU:1, one launch (start us, length us, event | category | flops | bytes accessed | tf_op | source)
XLA Modules:
  0.0 63.2 jit_solution(12015621570411972029)
XLA Ops:
  0.6 61.6 %step.1 = (bf16[16,16,1024]{2,1,0:T(8,128)(2,1)S(1)}, bf16[16,16,1024]{2,1,0:T(8,128)(2,1)S(1)}, f32[1,128]{1,0:T(1,128)S(1)}) custom-call(bf16[16,16,1024]{2,1,0:T(8,128)(2,1)} %state_ref.1, bf16[16,16,1024]{2,1,0:T(8,128)(2,1)} %cot_ref.1, bf16[2048,2048]{1,0:T(8,128)(2,1)} %coll_ref.1, f32[16,128]{1,0:T(8,128)} %bitcast.2, f32[16,128]{1,0:T(8,128)} %bitcast.3, ...), custom_call_target="tpu_custom_call" | custom-call | tf_op jit(solution)/shard_map/step/pallas_call | solution.py:340
  62.2 1.0 %write.1 = (bf16[16,16,1024]{2,1,0:T(8,128)(2,1)}, bf16[16,16,1024]{2,1,0:T(8,128)(2,1)}, f32[1,128]{1,0:T(1,128)}) custom-call(bf16[16,16,1024]{2,1,0:T(8,128)(2,1)S(1)} %get-tuple-element.6.a_ref, bf16[16,16,1024]{2,1,0:T(8,128)(2,1)S(1)} %get-tuple-element.7.b_ref, f32[1,128]{1,0:T(1,128)S(1)} %get-tuple-element.8.c_ref), custom_call_target="tpu_custom_call" | custom-call | tf_op jit(solution)/shard_map/write/pallas_call | solution.py:386

commit v4 on v3

--- a/solution.py
+++ b/solution.py
@@ -34,7 +34,7 @@
     svm, cvm, cmat, turn, halo_s, halo_g,
     cot_s, pas_s, adj_s, adv_s, cot_r, pas_r, adv_r,
     ws, wf, hbuf, xbuf, rt, coef, masks,
-    load_sem, send_sem, recv_sem, face_ss, face_rs,
+    load_sem, send_sem, recv_sem, face_ss, face_rs, line_ss, line_rs, cot_relay, pas_relay,
 ):
     me = lax.axis_index("vert")
     sa = lax.axis_index("sa")
@@ -78,7 +78,11 @@
     def greet(d):
         pl.semaphore_signal(barrier, inc=1, device_id={"vert": d}, device_id_type=MESH)
 
-    each_peer(greet)
+    my_col = my_y * 4 + my_x
+    for i in range(7):
+        greet(my_col * PER + far_z(i) * 2 + my_core)
+    for n in near[:-1]:
+        greet(n + my_z * 2)
     pl.semaphore_signal(barrier, inc=1, device_id={"sa": 1 - sa}, device_id_type=MESH)
     for c in loads[3:]:
         c.wait()
@@ -140,8 +144,55 @@
     def send_all(src, src_base, dst, dst_base, phase):
         each_peer(lambda d: send(src, src_base, dst, dst_base, phase, d))
 
-    def wait_blocks(ref, sem):
-        part = ref.at[pl.ds(0, NB - 1)]
+    def by_place(ref):
+        return ref.reshape(8, 8, 2, VL, LANES)
+
+    def send_line(src, relay, k):
+        def place(i, _):
+            z = far_z(i)
+            pltpu.make_async_remote_copy(
+                src_ref=by_place(src).at[:, z],
+                dst_ref=relay.at[my_z],
+                send_sem=line_ss.at[k],
+                recv_sem=line_rs.at[k, my_z],
+                device_id={"vert": my_col * PER + z * 2 + my_core},
+                device_id_type=MESH,
+            ).start()
+            return 0
+
+        lax.fori_loop(0, 7, place, 0)
+
+    def send_plane(part, dst, k, z):
+        for col in my_column:
+            for core in my_cores:
+                if col is my_column[-1] and core is my_cores[-1]:
+                    continue
+                pltpu.make_async_remote_copy(
+                    src_ref=part.at[col, core],
+                    dst_ref=by_place(dst).at[my_col, z, my_core],
+                    send_sem=send_sem.at[k],
+                    recv_sem=recv_sem.at[k],
+                    device_id={"vert": (col * 8 + my_z) * 2 + core},
+                    device_id_type=MESH,
+                ).start()
+        dst[(my_col * 8 + z) * 2 + my_core] = part[my_col, my_core]
+
+    def start_exchange(src, relay, dst, k):
+        send_line(src, relay, k)
+        send_plane(by_place(src).at[:, my_z], dst, k, my_z)
+
+    def relay_exchange(relay, dst, k):
+        def place(i, _):
+            z = far_z(i)
+            part = relay.at[z]
+            pltpu.make_async_copy(part, part, line_rs.at[k, z]).wait()
+            send_plane(part, dst, k, z)
+            return 0
+
+        lax.fori_loop(0, 7, place, 0)
+
+    def wait_blocks(ref, sem, blocks=NB - 1):
+        part = ref.at[pl.ds(0, blocks)]
         pltpu.make_async_copy(part, part, sem).wait()
 
     def face(buf, k):
@@ -197,14 +248,12 @@
 
     loads[0].wait()
     to_blocks(cvm, cot_s, 0)
+    pl.semaphore_wait(barrier, 23)
+    start_exchange(cot_s, cot_relay, cot_r, 0)
     loads[1].wait()
     to_blocks(svm, halo_s, YB)
-
-    pl.semaphore_wait(barrier, NB)
     face_s = face(halo_s, 0)
     face_s.start()
-    send_all(cot_s, 0, cot_r, 0, 0)
-    cot_r[me] = cot_s[me]
 
     face_s.wait()
 
@@ -212,8 +261,7 @@
         pas_s[x * YB + j] = res.astype(BF16)
 
     transport(halo_s, True, emit_passed)
-    send_all(pas_s, 0, pas_r, 0, 1)
-    pas_r[me] = pas_s[me]
+    start_exchange(pas_s, pas_relay, pas_r, 1)
 
     def spread(g, _):
         rows = pl.ds(pl.multiple_of(g * LANES, LANES), LANES)
@@ -235,7 +283,8 @@
         return jnp.sum(a.reshape(TILE // 8, 8, LANES), axis=0)
 
     loads[2].wait()
-    wait_blocks(cot_r, recv_sem.at[0])
+    relay_exchange(cot_relay, cot_r, 0)
+    wait_blocks(cot_r, recv_sem.at[0], NB - 8)
     cot_all = cot_r.reshape(2048, LANES)
 
     def adjoint_tile(t, total):
@@ -259,7 +308,8 @@
     send_all(adj_s, 0, halo_g, YB, 2)
     halo_g[YB + me] = adj_s[me]
 
-    wait_blocks(pas_r, recv_sem.at[1])
+    relay_exchange(pas_relay, pas_r, 1)
+    wait_blocks(pas_r, recv_sem.at[1], NB - 8)
     pas_all = pas_r.reshape(2048, LANES)
 
     def density_tile(t, total):
@@ -319,8 +369,11 @@
     lax.fori_loop(0, SLAB, unpack, 0, unroll=2)
     out_rows(adv_ref)
 
-    for phase, buf in enumerate((cot_s, pas_s, adj_s, adv_s)):
-        wait_blocks(buf, send_sem.at[phase])
+    for k, buf in enumerate((cot_s, pas_s)):
+        wait_blocks(buf, line_ss.at[k], NB - PER)
+        wait_blocks(buf, send_sem.at[k], NB - 8)
+    for k, buf in ((2, adj_s), (3, adv_s)):
+        wait_blocks(buf, send_sem.at[k])
 
 
 def write_kernel(a_ref, b_ref, c_ref, a_out, b_out, c_out, sems):
@@ -370,6 +423,10 @@
             pltpu.SemaphoreType.DMA((4,)),
             pltpu.SemaphoreType.DMA((2,)),
             pltpu.SemaphoreType.DMA((2,)),
+            pltpu.SemaphoreType.DMA((2,)),
+            pltpu.SemaphoreType.DMA((2, 8)),
+            pltpu.VMEM((8, 8, 2, VL, LANES), BF16),
+            pltpu.VMEM((8, 8, 2, VL, LANES), BF16),
         ],
         compiler_params=pltpu.CompilerParams(
             collective_id=0, has_side_effects=True, vmem_limit_bytes=32 * 1024 * 1024

time: 63.3 us -> 70 us (1.11)
  Pallas kernels: 62.6 us -> 69.2 us
    pallas_call x1, Pallas kernels: 61.6 us -> 68.3 us  [body(): pl.pallas_call(step_kernel, name='step', out_shape=(jax.ShapeDtypeStruct(...]
where the time goes in v4:
time: 70 us; the launch traced here: 69.9 us
  Pallas kernels  69.2 us (99%)
    pallas_call x1, Pallas kernels, body(): pl.pallas_call(step_kernel, name='step', out_shape=(jax.ShapeDtypeStruct(...  68.3 us

profile of v4, /device:TPU:1, one launch (start us, length us, event | category | flops | bytes accessed | tf_op | source)
XLA Modules:
  0.0 69.9 jit_solution(345220892021781572)
XLA Ops:
  0.6 68.3 %step.1 = (bf16[16,16,1024]{2,1,0:T(8,128)(2,1)S(1)}, bf16[16,16,1024]{2,1,0:T(8,128)(2,1)S(1)}, f32[1,128]{1,0:T(1,128)S(1)}) custom-call(bf16[16,16,1024]{2,1,0:T(8,128)(2,1)} %state_ref.1, bf16[16,16,1024]{2,1,0:T(8,128)(2,1)} %cot_ref.1, bf16[2048,2048]{1,0:T(8,128)(2,1)} %coll_ref.1, f32[16,128]{1,0:T(8,128)} %bitcast.2, f32[16,128]{1,0:T(8,128)} %bitcast.3, ...), custom_call_target="tpu_custom_call" | custom-call | tf_op jit(solution)/shard_map/step/pallas_call | solution.py:393
  68.9 1.0 %write.1 = (bf16[16,16,1024]{2,1,0:T(8,128)(2,1)}, bf16[16,16,1024]{2,1,0:T(8,128)(2,1)}, f32[1,128]{1,0:T(1,128)}) custom-call(bf16[16,16,1024]{2,1,0:T(8,128)(2,1)S(1)} %get-tuple-element.6.a_ref, bf16[16,16,1024]{2,1,0:T(8,128)(2,1)S(1)} %get-tuple-element.7.b_ref, f32[1,128]{1,0:T(1,128)S(1)} %get-tuple-element.8.c_ref), custom_call_target="tpu_custom_call" | custom-call | tf_op jit(solution)/shard_map/write/pallas_call | solution.py:443

commit v5 on v3

--- a/solution.py
+++ b/solution.py
@@ -34,7 +34,7 @@
     svm, cvm, cmat, turn, halo_s, halo_g,
     cot_s, pas_s, adj_s, adv_s, cot_r, pas_r, adv_r,
     ws, wf, hbuf, xbuf, rt, coef, masks,
-    load_sem, send_sem, recv_sem, face_ss, face_rs,
+    load_sem, send_sem, recv_sem, face_ss, face_rs, line_sem, all_in, relay,
 ):
     me = lax.axis_index("vert")
     sa = lax.axis_index("sa")
@@ -61,7 +61,7 @@
     def far_z(i):
         return (my_z + 4 + i // 2 - (i % 2) * i) % 8
 
-    def each_peer(visit):
+    def each_peer(visit, first=0):
         def place(i, _):
             z2 = far_z(i) * 2
             for n in near[:-1]:
@@ -73,12 +73,16 @@
 
             return 0
 
-        lax.fori_loop(0, 8, place, 0)
+        lax.fori_loop(first, 8, place, 0)
 
     def greet(d):
         pl.semaphore_signal(barrier, inc=1, device_id={"vert": d}, device_id_type=MESH)
 
-    each_peer(greet)
+    my_col = my_y * 4 + my_x
+    for i in range(7):
+        greet(my_col * PER + far_z(i) * 2 + my_core)
+    for n in near[:-1]:
+        greet(n + my_z * 2)
     pl.semaphore_signal(barrier, inc=1, device_id={"sa": 1 - sa}, device_id_type=MESH)
     for c in loads[3:]:
         c.wait()
@@ -137,11 +141,11 @@
 
         lax.fori_loop(0, 8, place, 0)
 
-    def send_all(src, src_base, dst, dst_base, phase):
-        each_peer(lambda d: send(src, src_base, dst, dst_base, phase, d))
-
-    def wait_blocks(ref, sem):
-        part = ref.at[pl.ds(0, NB - 1)]
+    def send_all(src, src_base, dst, dst_base, phase, first=0):
+        each_peer(lambda d: send(src, src_base, dst, dst_base, phase, d), first)
+
+    def wait_blocks(ref, sem, blocks=NB - 1):
+        part = ref.at[pl.ds(0, blocks)]
         pltpu.make_async_copy(part, part, sem).wait()
 
     def face(buf, k):
@@ -197,13 +201,27 @@
 
     loads[0].wait()
     to_blocks(cvm, cot_s, 0)
+
+    pl.semaphore_wait(barrier, 23)
+    for n in near[:-1]:
+        pl.semaphore_signal(all_in, inc=1, device_id={"vert": n + my_z * 2}, device_id_type=MESH)
+    z_far = (my_z + 4) % 8
+    line = pltpu.make_async_remote_copy(
+        src_ref=cot_s.reshape(8, 8, 2, VL, LANES).at[:, z_far],
+        dst_ref=relay,
+        send_sem=line_sem.at[0],
+        recv_sem=line_sem.at[1],
+        device_id={"vert": my_col * PER + z_far * 2 + my_core},
+        device_id_type=MESH,
+    )
+    line.start()
     loads[1].wait()
     to_blocks(svm, halo_s, YB)
-
-    pl.semaphore_wait(barrier, NB)
     face_s = face(halo_s, 0)
     face_s.start()
-    send_all(cot_s, 0, cot_r, 0, 0)
+
+    pl.semaphore_wait(all_in, 15)
+    send_all(cot_s, 0, cot_r, 0, 0, first=1)
     cot_r[me] = cot_s[me]
 
     face_s.wait()
@@ -212,6 +230,21 @@
         pas_s[x * YB + j] = res.astype(BF16)
 
     transport(halo_s, True, emit_passed)
+    line.wait()
+    came_from = my_col * PER + z_far * 2 + my_core
+    for col in my_column:
+        for core in my_cores:
+            if col is my_column[-1] and core is my_cores[-1]:
+                continue
+            pltpu.make_async_remote_copy(
+                src_ref=relay.at[col, core],
+                dst_ref=cot_r.at[came_from],
+                send_sem=send_sem.at[0],
+                recv_sem=recv_sem.at[0],
+                device_id={"vert": col * PER + my_z * 2 + core},
+                device_id_type=MESH,
+            ).start()
+    cot_r[came_from] = relay[my_col, my_core]
     send_all(pas_s, 0, pas_r, 0, 1)
     pas_r[me] = pas_s[me]
 
@@ -235,7 +268,7 @@
         return jnp.sum(a.reshape(TILE // 8, 8, LANES), axis=0)
 
     loads[2].wait()
-    wait_blocks(cot_r, recv_sem.at[0])
+    wait_blocks(cot_r, recv_sem.at[0], NB - 2)
     cot_all = cot_r.reshape(2048, LANES)
 
     def adjoint_tile(t, total):
@@ -320,7 +353,7 @@
     out_rows(adv_ref)
 
     for phase, buf in enumerate((cot_s, pas_s, adj_s, adv_s)):
-        wait_blocks(buf, send_sem.at[phase])
+        wait_blocks(buf, send_sem.at[phase], NB - 1 - (phase == 0))
 
 
 def write_kernel(a_ref, b_ref, c_ref, a_out, b_out, c_out, sems):
@@ -370,6 +403,9 @@
             pltpu.SemaphoreType.DMA((4,)),
             pltpu.SemaphoreType.DMA((2,)),
             pltpu.SemaphoreType.DMA((2,)),
+            pltpu.SemaphoreType.DMA((2,)),
+            pltpu.SemaphoreType.REGULAR,
+            pltpu.VMEM((8, 2, VL, LANES), BF16),
         ],
         compiler_params=pltpu.CompilerParams(
             collective_id=0, has_side_effects=True, vmem_limit_bytes=32 * 1024 * 1024

time: 63.3 us -> 62.6 us (0.989)
  Pallas kernels: 62.6 us -> 61.9 us
    pallas_call x1, Pallas kernels: 61.6 us -> 60.9 us  [body(): pl.pallas_call(step_kernel, name='step', out_shape=(jax.ShapeDtypeStruct(...]
where the time goes in v5:
time: 62.6 us
  Pallas kernels  61.9 us (99%)
  between operations  0.64 us (1%)
    pallas_call x1, Pallas kernels, body(): pl.pallas_call(step_kernel, name='step', out_shape=(jax.ShapeDtypeStruct(...  60.9 us

profile of v5, /device:TPU:1, one launch (start us, length us, event | category | flops | bytes accessed | tf_op | source)
XLA Modules:
  0.0 62.6 jit_solution(13116353941985816240)
XLA Ops:
  0.6 60.9 %step.1 = (bf16[16,16,1024]{2,1,0:T(8,128)(2,1)S(1)}, bf16[16,16,1024]{2,1,0:T(8,128)(2,1)S(1)}, f32[1,128]{1,0:T(1,128)S(1)}) custom-call(bf16[16,16,1024]{2,1,0:T(8,128)(2,1)} %state_ref.1, bf16[16,16,1024]{2,1,0:T(8,128)(2,1)} %cot_ref.1, bf16[2048,2048]{1,0:T(8,128)(2,1)} %coll_ref.1, f32[16,128]{1,0:T(8,128)} %bitcast.2, f32[16,128]{1,0:T(8,128)} %bitcast.3, ...), custom_call_target="tpu_custom_call" | custom-call | tf_op jit(solution)/shard_map/step/pallas_call | solution.py:373
  61.6 1.0 %write.1 = (bf16[16,16,1024]{2,1,0:T(8,128)(2,1)}, bf16[16,16,1024]{2,1,0:T(8,128)(2,1)}, f32[1,128]{1,0:T(1,128)}) custom-call(bf16[16,16,1024]{2,1,0:T(8,128)(2,1)S(1)} %get-tuple-element.6.a_ref, bf16[16,16,1024]{2,1,0:T(8,128)(2,1)S(1)} %get-tuple-element.7.b_ref, f32[1,128]{1,0:T(1,128)S(1)} %get-tuple-element.8.c_ref), custom_call_target="tpu_custom_call" | custom-call | tf_op jit(solution)/shard_map/write/pallas_call | solution.py:422

commit v6 on v5

--- a/solution.py
+++ b/solution.py
@@ -62,18 +62,19 @@
         return (my_z + 4 + i // 2 - (i % 2) * i) % 8
 
     def each_peer(visit, first=0):
-        def place(i, _):
-            z2 = far_z(i) * 2
-            for n in near[:-1]:
-                visit(z2 + n)
-
-            @pl.when(i < 7)
+        count = 8 - first
+
+        def turn_of(i, _):
+            for j, n in enumerate(near[:-1]):
+                visit(far_z(first + (i + j) % count) * 2 + n)
+
+            @pl.when((i + 15) % count < count - 1)
             def _():
-                visit(z2 + near[-1])
-
-            return 0
-
-        lax.fori_loop(first, 8, place, 0)
+                visit(far_z(first + (i + 15) % count) * 2 + near[-1])
+
+            return 0
+
+        lax.fori_loop(0, count, turn_of, 0)
 
     def greet(d):
         pl.semaphore_signal(barrier, inc=1, device_id={"vert": d}, device_id_type=MESH)

time: 62.6 us -> 63 us (level)
  no operation moved by 1% of the time
where the time goes in v6:
time: 63 us; the launch traced here: 62.9 us
  Pallas kernels  62.2 us (99%)
  between operations  0.64 us (1%)
    pallas_call x1, Pallas kernels, body(): pl.pallas_call(step_kernel, name='step', out_shape=(jax.ShapeDtypeStruct(...  61.2 us

profile of v6, /device:TPU:1, one launch (start us, length us, event | category | flops | bytes accessed | tf_op | source)
XLA Modules:
  0.0 62.9 jit_solution(9686542571230765397)
XLA Ops:
  0.6 61.2 %step.1 = (bf16[16,16,1024]{2,1,0:T(8,128)(2,1)S(1)}, bf16[16,16,1024]{2,1,0:T(8,128)(2,1)S(1)}, f32[1,128]{1,0:T(1,128)S(1)}) custom-call(bf16[16,16,1024]{2,1,0:T(8,128)(2,1)} %state_ref.1, bf16[16,16,1024]{2,1,0:T(8,128)(2,1)} %cot_ref.1, bf16[2048,2048]{1,0:T(8,128)(2,1)} %coll_ref.1, f32[16,128]{1,0:T(8,128)} %bitcast.2, f32[16,128]{1,0:T(8,128)} %bitcast.3, ...), custom_call_target="tpu_custom_call" | custom-call | tf_op jit(solution)/shard_map/step/pallas_call | solution.py:374
  61.9 1.0 %write.1 = (bf16[16,16,1024]{2,1,0:T(8,128)(2,1)}, bf16[16,16,1024]{2,1,0:T(8,128)(2,1)}, f32[1,128]{1,0:T(1,128)}) custom-call(bf16[16,16,1024]{2,1,0:T(8,128)(2,1)S(1)} %get-tuple-element.6.a_ref, bf16[16,16,1024]{2,1,0:T(8,128)(2,1)S(1)} %get-tuple-element.7.b_ref, f32[1,128]{1,0:T(1,128)S(1)} %get-tuple-element.8.c_ref), custom_call_target="tpu_custom_call" | custom-call | tf_op jit(solution)/shard_map/write/pallas_call | solution.py:423
